TPU v7x, 32 devices: a whole 2x2x4 slice. The times are simulated.
32 devices in a mesh: head: 4 (over y, x), ctx: 8 (over z, core).
Axes of the slice: x: 2, y: 2, z: 4, core: 2. Of those that a mesh axis runs over, the one named last changes fastest.
Arguments:
- query_rows: bfloat16 [4096, 2048], P(('ctx', 'head')), may hold values from -6 to 6
- key_rows: bfloat16 [4096, 2048], P(('ctx', 'head')), may hold values from -6 to 6
- value_rows: bfloat16 [4096, 4096], P(('ctx', 'head')), may hold values from -6 to 6
- gate_rows: bfloat16 [4096, 4096], P(('ctx', 'head')), may hold values from -6 to 6
- write_strength: bfloat16 [4096, 32], P(('ctx', 'head')), may hold values from 0 to 1
- log_decay: bfloat16 [4096, 32], P(('ctx', 'head')), may hold values from -1 to 0
- norm_gain: float32 [128], replicated, may hold values from 0.1 to 1.9
Outputs:
- mixed_out: bfloat16 [4096, 4096], P(('ctx', 'head'))
All inputs are finite; a program needn't handle non-finite values.
Results may differ from a plain program's by a relative error of at most 0.0049.
Values may be sent and summed in bfloat16 or wider, within the bound.
A program may use at most 192 MiB of HBM per device.

v0:
```python
import functools

import jax
import jax.numpy as jnp
from jax import lax
from jax.experimental import pallas as pl
from jax.experimental.pallas import tpu as pltpu
from jax.sharding import PartitionSpec as P

D = 128
B = 128
F32 = jnp.float32
BF = jnp.bfloat16
MESH = pl.DeviceIdType.MESH


def split(x):
    hi = x.astype(BF)
    return hi, (x - hi.astype(F32)).astype(BF)


def dot(a, b):
    return jnp.dot(a, b, preferred_element_type=F32)


def dot_t(a, b):
    return lax.dot_general(a, b, (((1,), (1,)), ((), ())), preferred_element_type=F32)


def dot_b(a, b):
    return dot(a.astype(BF), b.astype(BF))


def dot_fe(a, b):
    hi, lo = split(a)
    return dot(jnp.concatenate([hi, lo], 1), jnp.concatenate([b, b], 0))


def dot_ef(a, b):
    hi, lo = split(b)
    return dot(jnp.concatenate([a, a], 1), jnp.concatenate([hi, lo], 0))


def dot_ff(a, b):
    ah, al = split(a)
    bh, bl = split(b)
    return dot(jnp.concatenate([ah, ah], 1), jnp.concatenate([bh, bl], 0)) + dot(al, bh)


def exchange_kernel(n, q, k, v, be, de, qo, ko, vo, beo, deo, ssem, rsem, lsem):
    me = lax.axis_index("head")
    barrier = pltpu.get_barrier_semaphore()
    for s in range(1, n):
        pl.semaphore_signal(barrier, inc=1, device_id={"head": lax.rem(me + s, n)}, device_id_type=MESH)
    pl.semaphore_wait(barrier, n - 1)
    t = q.shape[0]
    rows = pl.ds(pl.multiple_of(me * t, t), t)
    arrays = [(de, deo, None), (be, beo, None), (k, ko, k.shape[1] // n), (v, vo, v.shape[1] // n), (q, qo, q.shape[1] // n)]

    def piece(src, dest, w):
        if w is None:
            return src
        return src.at[:, pl.ds(pl.multiple_of(dest * w, w), w)]

    copies = []
    for i, (src, dst, w) in enumerate(arrays):
        for s in range(1, n):
            dest = lax.rem(me + s, n)
            copies.append(
                pltpu.make_async_remote_copy(
                    src_ref=piece(src, dest, w),
                    dst_ref=dst.at[rows, :],
                    send_sem=ssem.at[i, s],
                    recv_sem=rsem.at[i, s],
                    device_id={"head": dest},
                    device_id_type=MESH,
                )
            )
            copies[-1].start()
    local = []
    for i, (src, dst, w) in enumerate(arrays):
        local.append(pltpu.make_async_copy(piece(src, me, w), dst.at[rows, :], lsem.at[i]))
        local[-1].start()
    for c in local:
        c.wait()
    for c in copies:
        c.wait()


def exchange(n, q, k, v, be, de):
    t = q.shape[0] * n
    any_spec = pl.BlockSpec(memory_space=pl.ANY)
    return pl.pallas_call(
        functools.partial(exchange_kernel, n),
        out_shape=[
            jax.ShapeDtypeStruct((t, q.shape[1] // n), BF),
            jax.ShapeDtypeStruct((t, k.shape[1] // n), BF),
            jax.ShapeDtypeStruct((t, v.shape[1] // n), BF),
            jax.ShapeDtypeStruct((t, be.shape[1]), BF),
            jax.ShapeDtypeStruct((t, de.shape[1]), BF),
        ],
        in_specs=[any_spec] * 5,
        out_specs=[any_spec] * 5,
        scratch_shapes=[
            pltpu.SemaphoreType.DMA((5, n)),
            pltpu.SemaphoreType.DMA((5, n)),
            pltpu.SemaphoreType.DMA((5,)),
        ],
        compiler_params=pltpu.CompilerParams(collective_id=0, has_side_effects=True),
    )(q, k, v, be, de)


def unit_lower_inverse(lows, ii, jj):
    eye = (ii == jj).astype(F32)

    def same(w):
        return (ii // w) == (jj // w)

    base = same(16)
    p = [jnp.where(base, -x, 0.0) for x in lows]
    t = [eye + x for x in p]
    for _ in range(3):
        pb = [x.astype(BF) for x in p]
        p = [dot(x, x) for x in pb]
        t = [y + dot_b(y, x) for y, x in zip(t, p)]
    w = 16
    while w < B:
        off = same(2 * w) & ~same(w)
        tb = [y.astype(BF) for y in t]
        z = [dot(jnp.where(off, x, 0.0).astype(BF), y) for x, y in zip(lows, tb)]
        t = [y - dot(yb, x.astype(BF)) for y, yb, x in zip(t, tb, z)]
        w *= 2
    return t


def block_kernel(heads, q_ref, k_ref, v_ref, be_ref, de_ref, base_ref, r_ref, x_ref):
    me = lax.axis_index("head")
    blocks = q_ref.shape[0] // B
    kheads = q_ref.shape[1] // D
    per = heads // kheads
    wide = be_ref.shape[1]
    ii = lax.broadcasted_iota(jnp.int32, (B, B), 0)
    jj = lax.broadcasted_iota(jnp.int32, (B, B), 1)
    eye = ii == jj
    causal = ii >= jj
    strict = ii > jj
    low = causal.astype(BF)
    upp = (ii <= jj).astype(BF)
    after = (ii < jj).astype(BF)
    ones = jnp.ones((B, B), BF)
    sel = (
        lax.broadcasted_iota(jnp.int32, (wide, heads), 0)
        == lax.broadcasted_iota(jnp.int32, (wide, heads), 1) + me * heads
    ).astype(BF)
    sel_t = (
        lax.broadcasted_iota(jnp.int32, (heads, wide), 1)
        == lax.broadcasted_iota(jnp.int32, (heads, wide), 0) + me * heads
    ).astype(BF)
    start = jnp.concatenate([jnp.zeros((B, D), F32), eye.astype(F32)], 1)
    for h in range(heads):
        x_ref[h] = start

    def one(b, carry):
        rows = pl.ds(pl.multiple_of(b * B, B), B)
        de = de_ref[rows, :]
        be = be_ref[rows, :]
        dcol = dot(de, sel).astype(BF)
        drow = dot_t(sel_t, de).astype(BF)
        bcol = dot(low, dcol)
        brow = dot(drow, upp)
        becol = dot(be, sel)
        berow = dot_t(sel_t, be)
        gcol = jnp.exp(bcol)
        grow = jnp.exp(brow)
        ecol = jnp.exp(dot(after, dcol))
        lastcol = jnp.exp(dot(ones, dcol))
        ks, qs, rkc, rkr, rqc, gn, hn = [], [], [], [], [], [], []
        for a in range(kheads):
            k = k_ref[rows, a * D : (a + 1) * D]
            q = q_ref[rows, a * D : (a + 1) * D]
            g = dot_t(k, k)
            diag = jnp.where(eye, g, 0.0)
            rc = lax.rsqrt(jnp.sum(diag, axis=1, keepdims=True) + 1e-6)
            rr = lax.rsqrt(jnp.sum(diag, axis=0, keepdims=True) + 1e-6)
            qf = q.astype(F32)
            qc = lax.rsqrt(jnp.sum(qf * qf, axis=1, keepdims=True) + 1e-6)
            ks.append(k)
            qs.append(q)
            rkc.append(rc)
            rkr.append(rr)
            rqc.append(qc)
            gn.append(g * rc * rr)
            hn.append(dot_t(q, k) * qc * rr)
        lows, reads = [], []
        for h in range(heads):
            a = h // per
            gap = bcol[:, h : h + 1] - brow[h : h + 1, :]
            wts = jnp.where(causal, jnp.exp(jnp.minimum(gap, 0.0)), 0.0)
            lows.append(jnp.where(strict, becol[:, h : h + 1] * wts * gn[a], 0.0))
            reads.append((wts * hn[a]).astype(BF))
        inv = unit_lower_inverse(lows, ii, jj)
        xs = [x_ref[h] for h in range(heads)]
        fresh, ds = [], []
        for h in range(heads):
            a = h // per
            br = berow[h : h + 1, :]
            u = dot_fe(inv[h] * br, v_ref[rows, h * D : (h + 1) * D])
            w = dot_fe(inv[h] * (br * grow[h : h + 1, :] * rkr[a]), ks[a])
            fresh.append(u)
            ds.append(w)
        for h in range(heads):
            ds[h] = jnp.concatenate([fresh[h], jnp.zeros((B, D), F32)], 1) - dot_ff(ds[h], xs[h])
        kts = [jnp.transpose(k) for k in ks]
        for h in range(heads):
            a = h // per
            x_ref[h] = lastcol[:, h : h + 1] * xs[h] + dot_ef(kts[a], (ecol[:, h : h + 1] * rkc[a]) * ds[h])
        for h in range(heads):
            a = h // per
            out = dot_ef(reads[h], ds[h]) + (gcol[:, h : h + 1] * rqc[a]) * dot_ef(qs[a], xs[h])
            base_ref[h, rows, :] = out[:, :D]
            r_ref[h, rows, :] = out[:, D:]
        return carry

    lax.fori_loop(0, blocks, one, 0)


def block_factors(heads, q, k, v, be, de):
    t = q.shape[0]
    spec = pl.BlockSpec(memory_space=pltpu.VMEM)
    return pl.pallas_call(
        functools.partial(block_kernel, heads),
        out_shape=[
            jax.ShapeDtypeStruct((heads, t, D), F32),
            jax.ShapeDtypeStruct((heads, t, D), F32),
            jax.ShapeDtypeStruct((heads, D, 2 * D), F32),
        ],
        in_specs=[spec] * 5,
        out_specs=[spec] * 3,
        compiler_params=pltpu.CompilerParams(vmem_limit_bytes=48 << 20),
    )(q, k, v, be, de)


def finish_kernel(n, m, heads, base, r, xf, gate, gain, out, sin, sout, core, got, cs, cr, ss, rs):
    me = lax.axis_index("head")
    c = lax.axis_index("ctx")
    t = gate.shape[0]
    barrier = pltpu.get_barrier_semaphore()
    for s in range(1, n):
        pl.semaphore_signal(barrier, inc=1, device_id={"head": lax.rem(me + s, n)}, device_id_type=MESH)

    for s in (1, m - 1):
        pl.semaphore_signal(barrier, inc=1, device_id={"ctx": lax.rem(c + s, m)}, device_id_type=MESH)
    pl.semaphore_wait(barrier, n + 1)

    def chain(h):
        return pltpu.make_async_remote_copy(
            src_ref=sout.at[h],
            dst_ref=sin.at[h],
            send_sem=cs.at[h],
            recv_sem=cr.at[h],
            device_id={"ctx": lax.rem(c + 1, m)},
            device_id_type=MESH,
        )

    def send(h, s):
        dest = lax.rem(me + s, n)
        return pltpu.make_async_remote_copy(
            src_ref=core.at[h, pl.ds(pl.multiple_of(dest * t, t), t), :],
            dst_ref=got.at[me * heads + h],
            send_sem=ss.at[h, s],
            recv_sem=rs.at[h, s],
            device_id={"head": dest},
            device_id_type=MESH,
        )

    def head_step(h, carry):
        @pl.when(c > 0)
        def _():
            chain(h).wait_recv()

        @pl.when(c == 0)
        def _():
            sin[h] = jnp.zeros((D, D), F32)

        state = sin[h]

        @pl.when(c < m - 1)
        def _():
            sout[h] = dot_ff(xf[h, :, D:], state) + xf[h, :, :D]
            chain(h).start()

        core[h] = (base[h] + dot_ff(r[h], state)).astype(BF)
        for s in range(1, n):
            send(h, s).start()
        got[me * heads + h] = core[h, pl.ds(pl.multiple_of(me * t, t), t), :]
        return carry

    lax.fori_loop(0, heads, head_step, 0)
    scale = gain[...]

    def norm(i):
        x = got[i].astype(F32)
        cols = pl.ds(pl.multiple_of(i * D, D), D)
        g = gate[:, cols].astype(F32)
        y = x * lax.rsqrt(jnp.mean(x * x, axis=-1, keepdims=True) + 1e-6)
        out[:, cols] = (y * scale * (g / (1.0 + jnp.exp(-g)))).astype(BF)

    def own(h, carry):
        norm(me * heads + h)
        return carry

    lax.fori_loop(0, heads, own, 0)

    def others(h, carry):
        for s in range(1, n):
            send(h, s).wait_recv()
            norm(lax.rem(me + n - s, n) * heads + h)
        return carry

    lax.fori_loop(0, heads, others, 0)

    def drain(h, carry):
        for s in range(1, n):
            send(h, s).wait_send()

        @pl.when(c < m - 1)
        def _():
            chain(h).wait_send()

        return carry

    lax.fori_loop(0, heads, drain, 0)


def finish(n, m, heads, base, r, xf, gate, gain):
    t, width = gate.shape
    spec = pl.BlockSpec(memory_space=pltpu.VMEM)
    return pl.pallas_call(
        functools.partial(finish_kernel, n, m, heads),
        out_shape=jax.ShapeDtypeStruct((t, width), BF),
        in_specs=[spec] * 5,
        out_specs=spec,
        scratch_shapes=[
            pltpu.VMEM((heads, D, D), F32),
            pltpu.VMEM((heads, D, D), F32),
            pltpu.VMEM((heads, t * n, D), BF),
            pltpu.VMEM((heads * n, t, D), BF),
            pltpu.SemaphoreType.DMA((heads,)),
            pltpu.SemaphoreType.DMA((heads,)),
            pltpu.SemaphoreType.DMA((heads, n)),
            pltpu.SemaphoreType.DMA((heads, n)),
        ],
        compiler_params=pltpu.CompilerParams(
            collective_id=1, has_side_effects=True, vmem_limit_bytes=48 << 20
        ),
    )(base, r, xf, gate, gain)


def solution(mesh):
    n, m = mesh.shape["head"], mesh.shape["ctx"]

    def local(q, k, v, gate, be, de, gain):
        heads = v.shape[1] // D // n
        q, k, v, be, de = exchange(n, q, k, v, be, de)
        base, r, xf = block_factors(heads, q, k, v, be, de)
        return finish(n, m, heads, base, r, xf, gate, gain.reshape(1, D))

    rows = P(("ctx", "head"), None)
    return jax.shard_map(
        local, mesh=mesh, in_specs=(rows,) * 6 + (P(),), out_specs=rows, check_vma=False
    )
```

profile of v0, /device:TPU:25, one launch (start us, length us, event | category | flops | bytes accessed | tf_op | source)
XLA Modules:
  0.0 85.7 jit_solution(451530330800185551)
XLA Ops:
  0.0 1.4 %copy.8.be = bf16[128,32]{1,0:T(8,128)(2,1)} copy(bf16[128,32]{0,1:T(8,128)(2,1)} %param.11) | data formatting | bytes 16384 | tf_op args[4]
  1.4 1.4 %copy.9.de = bf16[128,32]{1,0:T(8,128)(2,1)} copy(bf16[128,32]{0,1:T(8,128)(2,1)} %param.12) | data formatting | bytes 16384 | tf_op args[5]
  2.8 0.0 copy-start.1
  2.8 0.0 copy-start.6
  2.8 29.2 %shard_map.73 = (bf16[512,512]{1,0:T(8,128)(2,1)}, bf16[512,512]{1,0:T(8,128)(2,1)}, bf16[512,1024]{1,0:T(8,128)(2,1)}, bf16[512,32]{1,0:T(8,128)(2,1)}, bf16[512,32]{1,0:T(8,128)(2,1)}) custom-call(bf16[128,2048]{1,0:T(8,128)(2,1)} %q.1, bf16[128,2048]{1,0:T(8,128)(2,1)} %k.1, bf16[128,4096]{1,0:T(8,128)(2,1)} %v.1, bf16[128,32]{1,0:T(8,128)(2,1)} %copy.8.be, ...), custom_call_target="tpu_custom_call" | custom-call | tf_op jit(solution)/shard_map/pallas_call | solution.py:93
  32.0 0.0 copy-start
  32.0 1.2 %copy-done = bf16[512,1024]{1,0:T(8,128)(2,1)S(1)} copy-done((bf16[512,1024]{1,0:T(8,128)(2,1)S(1)}, bf16[512,1024]{1,0:T(8,128)(2,1)}, u32[]{:S(2)}) %copy-start) | copy-done | bytes 1048600
  33.2 0.0 copy-start.2
  33.2 1.0 %copy-done.2 = bf16[512,512]{1,0:T(8,128)(2,1)S(1)} copy-done((bf16[512,512]{1,0:T(8,128)(2,1)S(1)}, bf16[512,512]{1,0:T(8,128)(2,1)}, u32[]{:S(2)}) %copy-start.2) | copy-done | bytes 524312
  34.3 0.0 copy-start.3
  34.3 1.0 %copy-done.3 = bf16[512,512]{1,0:T(8,128)(2,1)S(1)} copy-done((bf16[512,512]{1,0:T(8,128)(2,1)S(1)}, bf16[512,512]{1,0:T(8,128)(2,1)}, u32[]{:S(2)}) %copy-start.3) | copy-done | bytes 524312
  35.3 0.0 copy-start.4
  35.3 0.9 %copy-done.4 = bf16[512,32]{1,0:T(8,128)(2,1)S(1)} copy-done((bf16[512,32]{1,0:T(8,128)(2,1)S(1)}, bf16[512,32]{1,0:T(8,128)(2,1)}, u32[]{:S(2)}) %copy-start.4) | copy-done | bytes 32792
  36.2 0.0 copy-start.5
  36.2 0.9 %copy-done.5 = bf16[512,32]{1,0:T(8,128)(2,1)S(1)} copy-done((bf16[512,32]{1,0:T(8,128)(2,1)S(1)}, bf16[512,32]{1,0:T(8,128)(2,1)}, u32[]{:S(2)}) %copy-start.5) | copy-done | bytes 32792
  37.1 16.4 %shard_map.74 = (f32[8,512,128]{2,1,0:T(8,128)S(1)}, f32[8,512,128]{2,1,0:T(8,128)}, f32[8,128,256]{2,1,0:T(8,128)S(1)}) custom-call(bf16[512,512]{1,0:T(8,128)(2,1)S(1)} %copy-done.2, bf16[512,512]{1,0:T(8,128)(2,1)S(1)} %copy-done.3, bf16[512,1024]{1,0:T(8,128)(2,1)S(1)} %copy-done, bf16[512,32]{1,0:T(8,128)(2,1)S(1)} %copy-done.4, ...), custom_call_target="tpu_custom_call" | custom-call | tf_op jit(solution)/shard_map/pallas_call | solution.py:230
  53.5 0.0 copy-done.1
  53.5 0.0 copy-done.6
  53.5 31.2 %shard_map.75 = bf16[128,4096]{1,0:T(8,128)(2,1)S(1)} custom-call(f32[8,512,128]{2,1,0:T(8,128)S(1)} %get-tuple-element.18.base, f32[8,512,128]{2,1,0:T(8,128)} %get-tuple-element.19.r, f32[8,128,256]{2,1,0:T(8,128)S(1)} %get-tuple-element.20.xf, bf16[128,4096]{1,0:T(8,128)(2,1)S(1)} %copy-done.1, f32[1,128]{1,0:T(1,128)S(1)} %bitcast.1), custom_call_target="tpu_custom_call" | custom-call | tf_op jit(solution)/shard_map/pallas_call | solution.py:338
  84.7 1.0 %copy.11 = bf16[128,4096]{1,0:T(8,128)(2,1)} copy(bf16[128,4096]{1,0:T(8,128)(2,1)S(1)} %shard_map.75) | data formatting | bytes 2097152
Async XLA Ops:
  2.8 50.7 %copy-start.1 = (bf16[128,4096]{1,0:T(8,128)(2,1)S(1)}, bf16[128,4096]{1,0:T(8,128)(2,1)}, u32[]{:S(2)}) copy-start(bf16[128,4096]{1,0:T(8,128)(2,1)} %gate.1) | copy-start | bytes 3145732
  2.8 50.7 %copy-start.6 = (f32[128]{0:T(128)S(1)}, f32[128]{0:T(128)}, u32[]{:S(2)}) copy-start(f32[128]{0:T(128)} %param.13) | copy-start | bytes 1540
  32.0 1.2 %copy-start = (bf16[512,1024]{1,0:T(8,128)(2,1)S(1)}, bf16[512,1024]{1,0:T(8,128)(2,1)}, u32[]{:S(2)}) copy-start(bf16[512,1024]{1,0:T(8,128)(2,1)} %get-tuple-element.15.v_ref) | copy-start | bytes 3145732
  33.2 1.0 %copy-start.2 = (bf16[512,512]{1,0:T(8,128)(2,1)S(1)}, bf16[512,512]{1,0:T(8,128)(2,1)}, u32[]{:S(2)}) copy-start(bf16[512,512]{1,0:T(8,128)(2,1)} %get-tuple-element.13.q_ref) | copy-start | bytes 1572868
  34.3 1.0 %copy-start.3 = (bf16[512,512]{1,0:T(8,128)(2,1)S(1)}, bf16[512,512]{1,0:T(8,128)(2,1)}, u32[]{:S(2)}) copy-start(bf16[512,512]{1,0:T(8,128)(2,1)} %get-tuple-element.14.k_ref) | copy-start | bytes 1572868
  35.3 0.9 %copy-start.4 = (bf16[512,32]{1,0:T(8,128)(2,1)S(1)}, bf16[512,32]{1,0:T(8,128)(2,1)}, u32[]{:S(2)}) copy-start(bf16[512,32]{1,0:T(8,128)(2,1)} %get-tuple-element.16.be_ref) | copy-start | bytes 98308
  36.2 0.9 %copy-start.5 = (bf16[512,32]{1,0:T(8,128)(2,1)S(1)}, bf16[512,32]{1,0:T(8,128)(2,1)}, u32[]{:S(2)}) copy-start(bf16[512,32]{1,0:T(8,128)(2,1)} %get-tuple-element.17.de_ref) | copy-start | bytes 98308
where the time goes:
time: 86.1 us; the launch traced here: 85.7 us
  Pallas kernels  76.7 us (89%)
  local copies, waits for them, and re-layouts  8.9 us (10%)
    pallas_call x1, Pallas kernels, finish(): pl.pallas_call(functools.partial(finish_kernel, n, m, heads), out_shape=j...  31.2 us
    pallas_call x1, Pallas kernels, exchange(): pl.pallas_call(functools.partial(exchange_kernel, n), out_shape=[jax.Shap...  29.2 us
    pallas_call x1, Pallas kernels, block_factors(): pl.pallas_call(functools.partial(block_kernel, heads), out_shape=[jax.Sha...  16.4 us
    unnamed x17, local copies, waits for them, and re-layouts  8.9 us

commit v1 on v0

v1 whole, which is shorter than its diff:
```python
import functools

import jax
import jax.numpy as jnp
from jax import lax
from jax.experimental import pallas as pl
from jax.experimental.pallas import tpu as pltpu
from jax.sharding import PartitionSpec as P

D = 128
B = 128
F32 = jnp.float32
BF = jnp.bfloat16
MESH = pl.DeviceIdType.MESH


def split(x):
    hi = x.astype(BF)
    return hi, (x - hi.astype(F32)).astype(BF)


def dot(a, b):
    return jnp.dot(a, b, preferred_element_type=F32)


def dot_t(a, b):
    return lax.dot_general(a, b, (((1,), (1,)), ((), ())), preferred_element_type=F32)


def dot_b(a, b):
    return dot(a.astype(BF), b.astype(BF))


def dot_fe(a, b):
    hi, lo = split(a)
    return dot(jnp.concatenate([hi, lo], 1), jnp.concatenate([b, b], 0))


def dot_ef(a, b):
    hi, lo = split(b)
    return dot(jnp.concatenate([a, a], 1), jnp.concatenate([hi, lo], 0))


def dot_ff(a, b):
    ah, al = split(a)
    bh, bl = split(b)
    return dot(jnp.concatenate([ah, ah], 1), jnp.concatenate([bh, bl], 0)) + dot(al, bh)


def unit_lower_inverse(lows, ii, jj):
    eye = (ii == jj).astype(F32)

    def same(w):
        return (ii // w) == (jj // w)

    base = same(16)
    p = [jnp.where(base, -x, 0.0) for x in lows]
    t = [eye + x for x in p]
    for _ in range(3):
        pb = [x.astype(BF) for x in p]
        p = [dot(x, x) for x in pb]
        t = [y + dot_b(y, x) for y, x in zip(t, p)]
    w = 16
    while w < B:
        off = same(2 * w) & ~same(w)
        tb = [y.astype(BF) for y in t]
        z = [dot(jnp.where(off, x, 0.0).astype(BF), y) for x, y in zip(lows, tb)]
        t = [y - dot(yb, x.astype(BF)) for y, yb, x in zip(t, tb, z)]
        w *= 2
    return t


def fused_kernel(
    n, m, kheads, per,
    q, k, v, be, de, gate_hbm, gain,
    out,
    qb, kb, vb, beb, deb, gate, xf, base, r, sin, sout, core, got,
    es, er, el, fs, fr, fl, gs, cs, cr, ss, rs,
):
    me = lax.axis_index("head")
    c = lax.axis_index("ctx")
    heads = kheads * per
    t = q.shape[0]
    wide = be.shape[0]
    blocks = t * n // B
    barrier = pltpu.get_barrier_semaphore()
    for s in range(1, n):
        pl.semaphore_signal(barrier, inc=1, device_id={"head": lax.rem(me + s, n)}, device_id_type=MESH)
    for s in (1, m - 1):
        pl.semaphore_signal(barrier, inc=1, device_id={"ctx": lax.rem(c + s, m)}, device_id_type=MESH)
    pl.semaphore_wait(barrier, n + 1)

    mine = pl.ds(pl.multiple_of(me * t, t), t)
    small = ((de, deb), (be, beb))
    large = ((k, kb, D), (v, vb, per * D), (q, qb, D))

    def small_copy(i, s):
        return pltpu.make_async_remote_copy(
            src_ref=small[i][0],
            dst_ref=small[i][1].at[me],
            send_sem=fs.at[i, s],
            recv_sem=fr.at[i, s],
            device_id={"head": lax.rem(me + s, n)},
            device_id_type=MESH,
        )

    def small_local(i):
        return pltpu.make_async_copy(small[i][0], small[i][1].at[me], fl.at[i])

    def piece(i, a, dest):
        w = large[i][2]
        return large[i][0].at[:, pl.ds(pl.multiple_of((dest * kheads + a) * w, w), w)]

    def large_copy(i, a, s):
        dest = lax.rem(me + s, n)
        return pltpu.make_async_remote_copy(
            src_ref=piece(i, a, dest),
            dst_ref=large[i][1].at[a, mine, :],
            send_sem=es.at[i, a, s],
            recv_sem=er.at[i, a, s],
            device_id={"head": dest},
            device_id_type=MESH,
        )

    def large_local(i, a):
        return pltpu.make_async_copy(piece(i, a, me), large[i][1].at[a, mine, :], el.at[i, a])

    for i in range(2):
        for s in range(1, n):
            small_copy(i, s).start()
        small_local(i).start()

    def begin(a, carry):
        for i in range(3):
            for s in range(1, n):
                large_copy(i, a, s).start()
            large_local(i, a).start()
        return carry

    lax.fori_loop(0, kheads, begin, 0)
    gate_copy = pltpu.make_async_copy(gate_hbm, gate, gs)
    gate_copy.start()

    ii = lax.broadcasted_iota(jnp.int32, (B, B), 0)
    jj = lax.broadcasted_iota(jnp.int32, (B, B), 1)
    eye = ii == jj
    causal = ii >= jj
    strict = ii > jj
    low = causal.astype(BF)
    upp = (ii <= jj).astype(BF)
    after = (ii < jj).astype(BF)
    ones = jnp.ones((B, B), BF)
    start = jnp.concatenate([jnp.zeros((B, D), F32), eye.astype(F32)], 1)
    for i in range(2):
        for s in range(1, n):
            small_copy(i, s).wait_recv()
        small_local(i).wait()

    def compute(a):
        for i in range(3):
            for s in range(1, n):
                large_copy(i, a, s).wait_recv()
            large_local(i, a).wait()
        first = (me * kheads + a) * per
        sel_t = (
            lax.broadcasted_iota(jnp.int32, (8, wide), 1)
            == lax.broadcasted_iota(jnp.int32, (8, wide), 0) + first
        ).astype(BF)
        lows, reads, rights, info = [], [], [], []
        for b in range(blocks):
            rows = slice(b * B, (b + 1) * B)
            here = slice((b * B) % t, (b * B) % t + B)
            drow = dot(sel_t, deb[b * B // t, :, here]).astype(BF)
            berow = dot(sel_t, beb[b * B // t, :, here])
            bcol = dot_t(low, drow)
            brow = dot(drow, upp)
            becol = dot_t(eye.astype(BF), berow.astype(BF))
            gcol = jnp.exp(bcol)
            grow = jnp.exp(brow)
            ecol = jnp.exp(dot_t(after, drow))
            lastcol = jnp.exp(dot_t(ones, drow))
            kk = kb[a, rows, :]
            qq = qb[a, rows, :]
            g = dot_t(kk, kk)
            diag = jnp.where(eye, g, 0.0)
            rc = lax.rsqrt(jnp.sum(diag, axis=1, keepdims=True) + 1e-6)
            rr = lax.rsqrt(jnp.sum(diag, axis=0, keepdims=True) + 1e-6)
            qf = qq.astype(F32)
            qc = lax.rsqrt(jnp.sum(qf * qf, axis=1, keepdims=True) + 1e-6)
            gn = g * rc * rr
            hn = dot_t(qq, kk) * qc * rr
            kt = jnp.transpose(kk)
            for u in range(per):
                gap = bcol[:, u : u + 1] - brow[u : u + 1, :]
                wts = jnp.where(causal, jnp.exp(jnp.minimum(gap, 0.0)), 0.0)
                lows.append(jnp.where(strict, becol[:, u : u + 1] * wts * gn, 0.0))
                reads.append((wts * hn).astype(BF))
                br = berow[u : u + 1, :]
                rights.append((br, br * grow[u : u + 1, :] * rr))
                info.append((kk, kt, qq, lastcol[:, u : u + 1], ecol[:, u : u + 1] * rc, gcol[:, u : u + 1] * qc))
        inv = unit_lower_inverse(lows, ii, jj)
        fresh, ws = [], []
        for b in range(blocks):
            for u in range(per):
                e = b * per + u
                fresh.append(dot_fe(inv[e] * rights[e][0], vb[a, b * B : (b + 1) * B, u * D : (u + 1) * D]))
                ws.append(dot_fe(inv[e] * rights[e][1], info[e][0]))
        xs = [start for u in range(per)]
        for b in range(blocks):
            rows = slice(b * B, (b + 1) * B)
            for u in range(per):
                e = b * per + u
                kk, kt, qq, last, end, read = info[e]
                d = jnp.concatenate([fresh[e], jnp.zeros((B, D), F32)], 1) - dot_ff(ws[e], xs[u])
                o = dot_ef(reads[e], d) + read * dot_ef(qq, xs[u])
                xs[u] = last * xs[u] + dot_ef(kt, end * d)
                base[a * per + u, rows, :] = o[:, :D]
                r[a * per + u, rows, :] = o[:, D:]
        for u in range(per):
            xf[a * per + u] = xs[u]

    def chain(h):
        return pltpu.make_async_remote_copy(
            src_ref=sout.at[h],
            dst_ref=sin.at[h],
            send_sem=cs.at[h],
            recv_sem=cr.at[h],
            device_id={"ctx": lax.rem(c + 1, m)},
            device_id_type=MESH,
        )

    def send(h, s):
        dest = lax.rem(me + s, n)
        return pltpu.make_async_remote_copy(
            src_ref=core.at[h, pl.ds(pl.multiple_of(dest * t, t), t), :],
            dst_ref=got.at[me * heads + h],
            send_sem=ss.at[h, s],
            recv_sem=rs.at[h, s],
            device_id={"head": dest},
            device_id_type=MESH,
        )

    def carry_on(a):
        for u in range(per):
            h = a * per + u

            @pl.when(c > 0)
            def _():
                chain(h).wait_recv()

            @pl.when(c == 0)
            def _():
                sin[h] = jnp.zeros((D, D), F32)

            @pl.when(c < m - 1)
            def _():
                sout[h] = dot_ff(xf[h, :, D:], sin[h]) + xf[h, :, :D]
                chain(h).start()

        for u in range(per):
            h = a * per + u
            core[h] = (base[h] + dot_ff(r[h], sin[h])).astype(BF)
            for s in range(1, n):
                send(h, s).start()
            got[me * heads + h] = core[h, mine, :]

    scale = gain[...]

    def norm(i):
        x = got[i].astype(F32)
        cols = pl.ds(pl.multiple_of(i * D, D), D)
        g = gate[:, cols].astype(F32)
        y = x * lax.rsqrt(jnp.mean(x * x, axis=-1, keepdims=True) + 1e-6)
        out[:, cols] = (y * scale * (g / (1.0 + jnp.exp(-g)))).astype(BF)

    def close(a):
        for u in range(per):
            h = a * per + u
            norm(me * heads + h)
            for s in range(1, n):
                send(h, s).wait_recv()
                norm(lax.rem(me + n - s, n) * heads + h)

    lag = jnp.minimum(c // 3, kheads - 1)

    def step(j, carry):
        @pl.when(j < kheads)
        def _():
            compute(j)

        now = j - lag

        @pl.when((now >= 0) & (now < kheads))
        def _():
            carry_on(now)

        @pl.when(now == 0)
        def _():
            gate_copy.wait()

        @pl.when((now >= 1) & (now <= kheads))
        def _():
            close(now - 1)

        return carry

    lax.fori_loop(0, 2 * kheads, step, 0)

    def drain(a, carry):
        for i in range(3):
            for s in range(1, n):
                large_copy(i, a, s).wait_send()
        for u in range(per):
            h = a * per + u
            for s in range(1, n):
                send(h, s).wait_send()

            @pl.when(c < m - 1)
            def _():
                chain(h).wait_send()

        return carry

    lax.fori_loop(0, kheads, drain, 0)
    for i in range(2):
        for s in range(1, n):
            small_copy(i, s).wait_send()


def solution(mesh):
    n, m = mesh.shape["head"], mesh.shape["ctx"]

    def local(q, k, v, gate, be, de, gain):
        t, width = v.shape
        heads = width // D // n
        kheads = k.shape[1] // D // n
        per = heads // kheads
        vm = pl.BlockSpec(memory_space=pltpu.VMEM)
        hbm = pl.BlockSpec(memory_space=pl.ANY)
        dma = pltpu.SemaphoreType.DMA
        return pl.pallas_call(
            functools.partial(fused_kernel, n, m, kheads, per),
            out_shape=jax.ShapeDtypeStruct((t, width), BF),
            in_specs=[hbm] * 6 + [vm],
            out_specs=vm,
            scratch_shapes=[
                pltpu.VMEM((kheads, t * n, D), BF),
                pltpu.VMEM((kheads, t * n, D), BF),
                pltpu.VMEM((kheads, t * n, per * D), BF),
                pltpu.VMEM((n, be.shape[1], t), BF),
                pltpu.VMEM((n, de.shape[1], t), BF),
                pltpu.VMEM((t, width), BF),
                pltpu.VMEM((heads, D, 2 * D), F32),
                pltpu.VMEM((heads, t * n, D), F32),
                pltpu.VMEM((heads, t * n, D), F32),
                pltpu.VMEM((heads, D, D), F32),
                pltpu.VMEM((heads, D, D), F32),
                pltpu.VMEM((heads, t * n, D), BF),
                pltpu.VMEM((heads * n, t, D), BF),
                dma((3, kheads, n)),
                dma((3, kheads, n)),
                dma((3, kheads)),
                dma((2, n)),
                dma((2, n)),
                dma((2,)),
                dma,
                dma((heads,)),
                dma((heads,)),
                dma((heads, n)),
                dma((heads, n)),
            ],
            compiler_params=pltpu.CompilerParams(
                collective_id=0, has_side_effects=True, vmem_limit_bytes=56 << 20
            ),
        )(q, k, v, be.T, de.T, gate, gain.reshape(1, D))

    rows = P(("ctx", "head"), None)
    return jax.shard_map(
        local, mesh=mesh, in_specs=(rows,) * 6 + (P(),), out_specs=rows, check_vma=False
    )
```

time: 86.1 us -> 68.6 us (0.80)
  Pallas kernels: 76.7 us -> 66.2 us
  local copies, waits for them, and re-layouts: 8.9 us -> 2.29 us
    pallas_call x3 -> x1, Pallas kernels: 76.7 us -> 66.2 us  [local(): pl.pallas_call(functools.partial(fused_kernel, n, m, kheads, per), out_sh...]
    unnamed x17 -> x1, local copies, waits for them, and re-layouts: 8.9 us -> 2.29 us
where the time goes in v1:
time: 68.6 us; the launch traced here: 68.5 us
  Pallas kernels  66.2 us (97%)
  local copies, waits for them, and re-layouts  2.29 us (3%)
    pallas_call x1, Pallas kernels, local(): pl.pallas_call(functools.partial(fused_kernel, n, m, kheads, per), out_sh...  66.2 us
    unnamed x1, local copies, waits for them, and re-layouts  2.29 us

profile of v1, /device:TPU:25, one launch (start us, length us, event | category | flops | bytes accessed | tf_op | source)
XLA Modules:
  0.0 68.5 jit_solution(15681280122206579076)
XLA Ops:
  0.0 66.2 %shard_map.73 = bf16[128,4096]{1,0:T(8,128)(2,1)} custom-call(bf16[128,2048]{1,0:T(8,128)(2,1)} %q.1, bf16[128,2048]{1,0:T(8,128)(2,1)} %k.1, bf16[128,4096]{1,0:T(8,128)(2,1)} %v.1, bf16[32,128]{1,0:T(8,128)(2,1)} %bitcast.3, bf16[32,128]{1,0:T(8,128)(2,1)} %bitcast.4, bf16[128,4096]{1,0:T(8,128)(2,1)} %gate_hbm.1, f32[1,128]{1,0:T(1,128)} %bitcast.5), custom_call_target="tpu_custom_call" | custom-call | tf_op jit(solution)/shard_map/pallas_call | solution.py:341
  66.2 2.3 %copy.9 = bf16[128,4096]{1,0:T(8,128)(2,1)} copy(bf16[128,4096]{1,0:T(8,128)(2,1)} %shard_map.73) | data formatting | bytes 2097152

commit v2 on v1

--- a/solution.py
+++ b/solution.py
@@ -150,7 +150,6 @@
     upp = (ii <= jj).astype(BF)
     after = (ii < jj).astype(BF)
     ones = jnp.ones((B, B), BF)
-    start = jnp.concatenate([jnp.zeros((B, D), F32), eye.astype(F32)], 1)
     for i in range(2):
         for s in range(1, n):
             small_copy(i, s).wait_recv()
@@ -199,25 +198,43 @@
                 rights.append((br, br * grow[u : u + 1, :] * rr))
                 info.append((kk, kt, qq, lastcol[:, u : u + 1], ecol[:, u : u + 1] * rc, gcol[:, u : u + 1] * qc))
         inv = unit_lower_inverse(lows, ii, jj)
-        fresh, ws = [], []
+        zero = jnp.zeros((B, D), F32)
+        uws = []
         for b in range(blocks):
             for u in range(per):
                 e = b * per + u
-                fresh.append(dot_fe(inv[e] * rights[e][0], vb[a, b * B : (b + 1) * B, u * D : (u + 1) * D]))
-                ws.append(dot_fe(inv[e] * rights[e][1], info[e][0]))
-        xs = [start for u in range(per)]
+                vv = vb[a, b * B : (b + 1) * B, u * D : (u + 1) * D]
+                uws.append(
+                    jnp.concatenate(
+                        [dot_fe(inv[e] * rights[e][0], vv), dot_fe(inv[e] * rights[e][1], info[e][0])], 1
+                    )
+                )
+        steps = []
+        for e, uw in enumerate(uws):
+            kk, kt, qq, last, end, read = info[e]
+            tw = dot_ef(kt, end * uw)
+            steps.append((tw[:, :D], jnp.where(eye, last, 0.0) - tw[:, D:]))
+        xs = [[jnp.concatenate(steps[u], 1)] for u in range(per)]
+        for b in range(1, blocks):
+            for u in range(per):
+                written, trans = steps[b * per + u]
+                xs[u].append(dot_ff(trans, xs[u][-1]) + jnp.concatenate([written, zero], 1))
+        for u in range(per):
+            xf[a * per + u] = xs[u][-1]
         for b in range(blocks):
             rows = slice(b * B, (b + 1) * B)
             for u in range(per):
                 e = b * per + u
                 kk, kt, qq, last, end, read = info[e]
-                d = jnp.concatenate([fresh[e], jnp.zeros((B, D), F32)], 1) - dot_ff(ws[e], xs[u])
-                o = dot_ef(reads[e], d) + read * dot_ef(qq, xs[u])
-                xs[u] = last * xs[u] + dot_ef(kt, end * d)
-                base[a * per + u, rows, :] = o[:, :D]
-                r[a * per + u, rows, :] = o[:, D:]
-        for u in range(per):
-            xf[a * per + u] = xs[u]
+                lr = dot_ef(reads[e], uws[e])
+                near = lr[:, :D]
+                far = read * qq.astype(F32) - lr[:, D:]
+                if b > 0:
+                    o = dot_ef(far.astype(BF), xs[u][b - 1])
+                    near = near + o[:, :D]
+                    far = o[:, D:]
+                base[a * per + u, rows, :] = near
+                r[a * per + u, rows, :] = far.astype(BF)
 
     def chain(h):
         return pltpu.make_async_remote_copy(
@@ -259,7 +276,7 @@
 
         for u in range(per):
             h = a * per + u
-            core[h] = (base[h] + dot_ff(r[h], sin[h])).astype(BF)
+            core[h] = (base[h] + dot_ef(r[h], sin[h])).astype(BF)
             for s in range(1, n):
                 send(h, s).start()
             got[me * heads + h] = core[h, mine, :]
@@ -352,7 +369,7 @@
                 pltpu.VMEM((t, width), BF),
                 pltpu.VMEM((heads, D, 2 * D), F32),
                 pltpu.VMEM((heads, t * n, D), F32),
-                pltpu.VMEM((heads, t * n, D), F32),
+                pltpu.VMEM((heads, t * n, D), BF),
                 pltpu.VMEM((heads, D, D), F32),
                 pltpu.VMEM((heads, D, D), F32),
                 pltpu.VMEM((heads, t * n, D), BF),

time: 68.6 us -> 66.6 us (0.971)
  Pallas kernels: 66.2 us -> 64.1 us
    pallas_call x1, Pallas kernels: 66.2 us -> 64.1 us  [local(): pl.pallas_call(functools.partial(fused_kernel, n, m, kheads, per), out_sh...]
where the time goes in v2:
time: 66.6 us; the launch traced here: 66.4 us
  Pallas kernels  64.1 us (96%)
  local copies, waits for them, and re-layouts  2.29 us (3%)
    pallas_call x1, Pallas kernels, local(): pl.pallas_call(functools.partial(fused_kernel, n, m, kheads, per), out_sh...  64.1 us
    unnamed x1, local copies, waits for them, and re-layouts  2.29 us

profile of v2, /device:TPU:25, one launch (start us, length us, event | category | flops | bytes accessed | tf_op | source)
XLA Modules:
  0.0 66.4 jit_solution(9086229154061738173)
XLA Ops:
  0.0 64.1 %shard_map.73 = bf16[128,4096]{1,0:T(8,128)(2,1)} custom-call(bf16[128,2048]{1,0:T(8,128)(2,1)} %q.1, bf16[128,2048]{1,0:T(8,128)(2,1)} %k.1, bf16[128,4096]{1,0:T(8,128)(2,1)} %v.1, bf16[32,128]{1,0:T(8,128)(2,1)} %bitcast.3, bf16[32,128]{1,0:T(8,128)(2,1)} %bitcast.4, bf16[128,4096]{1,0:T(8,128)(2,1)} %gate_hbm.1, f32[1,128]{1,0:T(1,128)} %bitcast.5), custom_call_target="tpu_custom_call" | custom-call | tf_op jit(solution)/shard_map/pallas_call | solution.py:358
  64.1 2.3 %copy.9 = bf16[128,4096]{1,0:T(8,128)(2,1)} copy(bf16[128,4096]{1,0:T(8,128)(2,1)} %shard_map.73) | data formatting | bytes 2097152
